TPU v7x, 32 devices: a whole 2x2x4 slice. The times are simulated.
32 devices in a mesh: group: 2 (over y), head: 4 (over z), cache: 4 (over x, core).
Axes of the slice: x: 2, y: 2, z: 4, core: 2. Of those that a mesh axis runs over, the one named last changes fastest.
Arguments:
- queries: bfloat16 [512, 4096], P(('group', 'head')), parts along dimension 0, may hold values from -8 to 8
- keys: bfloat16 [256, 128, 4096], P(('group', 'cache'), None, 'head'), parts along dimension 0, may hold values from -8 to 8
- values: bfloat16 [256, 128, 4096], P(('group', 'cache'), None, 'head'), parts along dimension 0, may hold values from -6 to 6
- page_lists: int32 [8, 32], P(('group', 'cache')), parts along dimension 0, may hold values from 0 to 31, as said below
- page_counts: int32 [8], P(('group', 'cache')), parts along dimension 0, may hold values from 1 to 32, as said below
Outputs:
- attended: float32 [512, 4096], P(('group', 'head', 'cache')), parts along dimension 0
- log_sums: float32 [512, 32], P(('group', 'head', 'cache')), parts along dimension 0
There are 2 independent parts, one for each index of `group`. A program takes and returns all parts, laid end to end along the dimension named above; each array names one. Nothing has to cross between parts.
Inputs may be any that keep to these rules, and one draw needn't show every extreme that they name: `page_lists`: row c holds 32 distinct page ids of owner c's pool; only its first page_counts[c] entries are attended. `page_counts`: some owner lists exactly 32 pages in every draw.
All inputs are finite; a program needn't handle non-finite values.
Results may differ from a plain program's by a relative error of at most 0.00038.
Values may be sent and summed in bfloat16 or wider, within the bound.
A program may use at most 64 MiB of HBM per device.

v0:
```python
import functools
import math

import jax
import jax.numpy as jnp
from jax import lax
from jax.experimental import pallas as pl
from jax.experimental.pallas import tpu as pltpu
from jax.sharding import PartitionSpec as P

DH = 128
PAGE = 128
LANES = 128
TILE = 256
ROWS = DH + 8
BLOCK = 8
SCALE = 1.0 / math.sqrt(DH)
LOG2_SCALE = SCALE * math.log2(math.e)

lowest = -1e30
highest = 3e38


def attend(queries, key_of, value_of, caps, pages, acc, scores):
    units = len(queries)
    acc[...] = jnp.zeros_like(acc)
    ones = jnp.ones((16, PAGE), jnp.bfloat16)
    blocks = pages // BLOCK

    def score(unit, page):
        rows = key_of(unit, pl.ds(page, BLOCK)).reshape(BLOCK * PAGE, DH)
        return lax.dot_general(
            rows, queries[unit][...], (((1,), (1,)), ((), ())),
            preferred_element_type=jnp.float32,
        ).reshape(BLOCK, PAGE, TILE)

    for unit in range(units):
        scores[unit] = score(unit, 0)

    def visit(block, bests, more=True):
        runnings = []
        for unit in range(units):
            maxima, outs = [], []
            for step in range(BLOCK):
                page = block * BLOCK + step
                page_max = jnp.max(scores[unit, step], axis=0, keepdims=True)
                weights = jnp.exp2((scores[unit, step] - page_max) * LOG2_SCALE).astype(jnp.bfloat16)
                left = jnp.concatenate([value_of(unit, page).T, ones], axis=0)
                outs.append(jnp.dot(left, weights, preferred_element_type=jnp.float32)[:ROWS])
                maxima.append(jnp.minimum(page_max, caps[pl.ds(page, 1), :]))
            if more:
                scores[unit] = score(unit, (block + 1) * BLOCK)
            running = functools.reduce(jnp.maximum, maxima, bests[unit])
            joined = acc[unit] * jnp.exp2((bests[unit] - running) * LOG2_SCALE)
            for used_max, out in zip(maxima, outs):
                joined += out * jnp.exp2((used_max - running) * LOG2_SCALE)
            acc[unit] = joined
            runnings.append(running)
        return tuple(runnings)

    start = jnp.full((1, TILE), lowest, jnp.float32)
    bests = lax.fori_loop(0, blocks - 1, visit, (start,) * units)
    return visit(blocks - 1, bests, more=False)


def kernel(
    plan, q_ref, k_hbm, v_hbm, lists, counts, out_ref, log_ref,
    caps, k_buf, v_buf, q_all, q_units, acc, scores, part_out, part_in, piece_out, piece_in, log_out, log_in,
    k_sem, v_sem, own_sem, q_send, q_recv, part_send, part_recv, piece_send, piece_recv, log_send, log_recv,
):
    groups, heads_in, tiles_in, tile_blocks, n_head, n_cache, heads, sources = plan
    units = heads_in * tiles_in
    width = heads_in * DH
    pages = k_hbm.shape[0]
    head_blocks = groups // tile_blocks
    share = q_ref.shape[0] // n_cache
    chunk = TILE // n_cache
    spread = tiles_in * sources
    me = lax.axis_index("head")
    seat = lax.axis_index("cache")

    def load(block):
        columns = pl.ds(pl.multiple_of(block * width, DH), width)
        return (
            pltpu.make_async_copy(k_hbm.at[:, :, columns], k_buf.at[block], k_sem.at[block]),
            pltpu.make_async_copy(v_hbm.at[:, :, columns], v_buf.at[block], v_sem.at[block]),
        )

    def peer_of(index, count, offset):
        return lax.rem(index + offset, count)

    def query_source(block, owner):
        return q_ref.at[:, pl.ds(pl.multiple_of(owner * heads * DH + block * width, DH), width)]

    def own_query(block):
        return pltpu.make_async_copy(query_source(block, me), q_all.at[block, me], own_sem.at[block])

    def query_copy(block, offset, source):
        peer = peer_of(me, n_head, offset)
        return pltpu.make_async_remote_copy(
            src_ref=query_source(block, peer), dst_ref=q_all.at[block, source],
            send_sem=q_send.at[block, offset - 1], recv_sem=q_recv.at[block, source],
            device_id={"head": peer}, device_id_type=pl.DeviceIdType.MESH,
        )

    def part_copy(group, offset, source):
        peer = peer_of(seat, n_cache, offset)
        return pltpu.make_async_remote_copy(
            src_ref=part_out.at[group, peer], dst_ref=part_in.at[group, source],
            send_sem=part_send.at[group, offset - 1], recv_sem=part_recv.at[group, source],
            device_id={"cache": peer}, device_id_type=pl.DeviceIdType.MESH,
        )

    def piece_copy(group, place, source):
        target = group % tile_blocks * spread + place
        block = group // tile_blocks
        return target, pltpu.make_async_remote_copy(
            src_ref=piece_out.at[group, place], dst_ref=piece_in.at[block, source],
            send_sem=piece_send.at[group, place], recv_sem=piece_recv.at[block, source],
            device_id={"head": target}, device_id_type=pl.DeviceIdType.MESH,
        )

    def log_copy(offset, source):
        peer = peer_of(me, n_head, offset)
        return pltpu.make_async_remote_copy(
            src_ref=log_out.at[peer], dst_ref=log_in.at[source],
            send_sem=log_send.at[offset - 1], recv_sem=log_recv.at[source],
            device_id={"head": peer}, device_id_type=pl.DeviceIdType.MESH,
        )

    for copy in load(0):
        copy.start()
    barrier = pltpu.get_barrier_semaphore()
    for offset in range(1, n_head):
        pl.semaphore_signal(
            barrier, inc=1, device_id={"head": peer_of(me, n_head, offset)},
            device_id_type=pl.DeviceIdType.MESH,
        )
    for offset in range(1, n_cache):
        pl.semaphore_signal(
            barrier, inc=1, device_id={"cache": peer_of(seat, n_cache, offset)},
            device_id_type=pl.DeviceIdType.MESH,
        )
    for block in range(head_blocks):
        own_query(block).start()
    pl.semaphore_wait(barrier, n_head + n_cache - 2)
    for offset in range(1, n_head):
        query_copy(0, offset, me).start()
    log_out[...] = jnp.zeros_like(log_out)
    slots = lists.shape[1]
    used = lax.broadcasted_iota(jnp.int32, (1, slots), 1) < counts[0]
    listed = jnp.where(used, lists[...], -1)
    match = listed == lax.broadcasted_iota(jnp.int32, (pages, slots), 0)
    cap = jnp.max(jnp.where(match, highest, lowest), axis=1, keepdims=True)
    caps[...] = jnp.broadcast_to(cap, caps.shape)

    def ready(block):
        for copy in load(block):
            copy.wait()
        own_query(block).wait()
        for offset in range(1, n_head):
            query_copy(block, offset, peer_of(me, n_head, offset)).wait_recv()

        @pl.when(block + 1 < head_blocks)
        def _():
            for copy in load(block + 1):
                copy.start()
            for offset in range(1, n_head):
                query_copy(block + 1, offset, me).start()

    def compute(group):
        block = group // tile_blocks
        if tile_blocks == 1:
            ready(block)
        else:
            pl.when(group % tile_blocks == 0)(lambda: ready(block))

        def column(unit):
            return slice(unit // tiles_in * DH, (unit // tiles_in + 1) * DH)

        for unit in range(units):
            first = (group % tile_blocks * tiles_in + unit % tiles_in) * sources
            rows = [q_all[block, first + l, :, column(unit)].astype(jnp.float32) for l in range(sources)]
            ordered = [
                row[c * share:(c + 1) * share] for c in range(n_cache) for row in rows
            ]
            q_units[unit] = jnp.concatenate(ordered, axis=0).astype(jnp.bfloat16)
        bests = attend(
            [q_units.at[unit] for unit in range(units)],
            lambda unit, page: k_buf[block, page, :, column(unit)],
            lambda unit, page: v_buf[block, page, :, column(unit)],
            caps, pages, acc, scores,
        )
        row = lax.broadcasted_iota(jnp.int32, (8, TILE), 0)
        tails = [jnp.where(row == 1, best, acc[unit, DH:ROWS]) for unit, best in enumerate(bests)]
        for member in range(n_cache):
            piece = slice(member * chunk, (member + 1) * chunk)
            part_out[group, member, :DH] = jnp.concatenate(
                [acc[unit, :DH, piece] for unit in range(units)], axis=1
            )
            part_out[group, member, DH:ROWS] = jnp.concatenate([tail[:, piece] for tail in tails], axis=1)
        for offset in range(1, n_cache):
            part_copy(group, offset, seat).start()
        part_in[group, seat] = part_out[group, seat]

    def finish(group):
        block = group // tile_blocks
        for offset in range(1, n_cache):
            part_copy(group, offset, peer_of(seat, n_cache, offset)).wait_recv()
        totals = [part_in[group, c, DH:DH + 1] for c in range(n_cache)]
        bests = [part_in[group, c, DH + 1:DH + 2] for c in range(n_cache)]
        top = functools.reduce(jnp.maximum, bests)
        keeps = [jnp.exp2((best - top) * LOG2_SCALE) for best in bests]
        total = functools.reduce(jnp.add, [t * keep for t, keep in zip(totals, keeps)])
        inverse = 1.0 / total
        result = functools.reduce(
            jnp.add, [part_in[group, c, :DH] * (keep * inverse) for c, keep in enumerate(keeps)]
        ).T
        logged = jnp.broadcast_to(top * SCALE + jnp.log(total), (LANES, LANES)).T
        lane = lax.broadcasted_iota(jnp.int32, (share, LANES), 1)
        for unit in range(units):
            head = unit // tiles_in
            for l in range(sources):
                place = unit % tiles_in * sources + l
                at = unit * sources * share + l * share
                piece_out[group, place, :, head * DH:(head + 1) * DH] = result[at:at + share]
                target = group % tile_blocks * spread + place
                log_out[target] += jnp.where(
                    lane == me * heads + block * heads_in + head, logged[at:at + share], 0.0
                )
        for place in range(spread):
            target, copy = piece_copy(group, place, me)
            pl.when(target != me)(copy.start)

            @pl.when(target == me)
            def _():
                piece_in[block, me] = piece_out[group, place]

    def step(group, carry):
        compute(group)
        pl.when(group > 0)(lambda: finish(group - 1))
        return carry

    lax.fori_loop(0, groups, step, 0)
    finish(groups - 1)
    for offset in range(1, n_head):
        log_copy(offset, me).start()
    log_in[me] = log_out[me]
    for block in range(head_blocks):
        for offset in range(1, n_head):
            query_copy(block, offset, me).wait_send()
    for group in range(groups):
        for offset in range(1, n_cache):
            part_copy(group, offset, seat).wait_send()
    for block in range(head_blocks):
        for offset in range(1, n_head):
            source = peer_of(me, n_head, offset)
            pltpu.make_async_remote_copy(
                src_ref=piece_out.at[block, 0], dst_ref=piece_in.at[block, source],
                send_sem=piece_send.at[block, 0], recv_sem=piece_recv.at[block, source],
                device_id={"head": source}, device_id_type=pl.DeviceIdType.MESH,
            ).wait_recv()
        for source in range(n_head):
            at = (source * heads + block * heads_in) * DH
            out_ref[:, at:at + width] = piece_in[block, source]
    for offset in range(1, n_head):
        log_copy(offset, peer_of(me, n_head, offset)).wait_recv()
    log_ref[...] = functools.reduce(jnp.add, [log_in[s] for s in range(n_head)])[:, :log_ref.shape[1]]
    for group in range(groups):
        for place in range(spread):
            target, copy = piece_copy(group, place, me)
            pl.when(target != me)(copy.wait_send)
    for offset in range(1, n_head):
        log_copy(offset, me).wait_send()


def on_device(queries, keys, values, page_lists, page_counts):
    n_head = lax.axis_size("head")
    n_cache = lax.axis_size("cache")
    tok_local = queries.shape[0]
    heads = keys.shape[2] // DH
    pages = keys.shape[0]
    share = tok_local // n_cache
    sources = TILE // tok_local
    tiles = n_head // sources
    units = LANES * n_cache // TILE
    tiles_in = min(units, tiles)
    heads_in = units // tiles_in
    tile_blocks = tiles // tiles_in
    head_blocks = heads // heads_in
    groups = head_blocks * tile_blocks
    spread = tiles_in * sources
    width = heads_in * DH
    plan = (groups, heads_in, tiles_in, tile_blocks, n_head, n_cache, heads, sources)
    dma = pltpu.SemaphoreType.DMA
    attended, logged = pl.pallas_call(
        functools.partial(kernel, plan),
        out_shape=(
            pltpu.VMEM((share, queries.shape[1]), jnp.float32),
            pltpu.VMEM((share, n_head * heads), jnp.float32),
        ),
        in_specs=[
            pl.BlockSpec(memory_space=pltpu.VMEM),
            pl.BlockSpec(memory_space=pl.ANY),
            pl.BlockSpec(memory_space=pl.ANY),
            pl.BlockSpec(memory_space=pltpu.VMEM),
            pl.BlockSpec(memory_space=pltpu.SMEM),
        ],
        out_specs=(pl.BlockSpec(memory_space=pltpu.VMEM), pl.BlockSpec(memory_space=pltpu.VMEM)),
        scratch_shapes=[
            pltpu.VMEM((pages, TILE), jnp.float32),
            pltpu.VMEM((head_blocks, pages, PAGE, width), jnp.bfloat16),
            pltpu.VMEM((head_blocks, pages, PAGE, width), jnp.bfloat16),
            pltpu.VMEM((head_blocks, n_head, tok_local, width), jnp.bfloat16),
            pltpu.VMEM((units, TILE, DH), jnp.bfloat16),
            pltpu.VMEM((units, ROWS, TILE), jnp.float32),
            pltpu.VMEM((units, BLOCK, PAGE, TILE), jnp.float32),
            pltpu.VMEM((groups, n_cache, ROWS, LANES), jnp.float32),
            pltpu.VMEM((groups, n_cache, ROWS, LANES), jnp.float32),
            pltpu.VMEM((groups, spread, share, width), jnp.float32),
            pltpu.VMEM((head_blocks, n_head, share, width), jnp.float32),
            pltpu.VMEM((n_head, share, LANES), jnp.float32),
            pltpu.VMEM((n_head, share, LANES), jnp.float32),
            dma((head_blocks,)),
            dma((head_blocks,)),
            dma((head_blocks,)),
            dma((head_blocks, n_head - 1)),
            dma((head_blocks, n_head)),
            dma((groups, n_cache - 1)),
            dma((groups, n_cache)),
            dma((groups, spread)),
            dma((head_blocks, n_head)),
            dma((n_head - 1,)),
            dma((n_head,)),
        ],
        compiler_params=pltpu.CompilerParams(
            collective_id=0, has_side_effects=True, vmem_limit_bytes=56 * 1024 * 1024
        ),
    )(queries, keys, values, page_lists, page_counts)
    return attended, logged


def solution(mesh):
    in_specs = (
        P(("group", "head"), None),
        P(("group", "cache"), None, "head"),
        P(("group", "cache"), None, "head"),
        P(("group", "cache"), None),
        P(("group", "cache")),
    )
    out_specs = (P(("group", "head", "cache"), None), P(("group", "head", "cache"), None))
    return jax.shard_map(
        on_device, mesh=mesh, in_specs=in_specs, out_specs=out_specs, check_vma=False
    )
```

profile of v0, /device:TPU:0, one launch (start us, length us, event | category | flops | bytes accessed | tf_op | source)
XLA Modules:
  0.0 39.3 jit_solution(4520985504636051178)
XLA Ops:
  1.3 36.7 %shard_map.68 = (f32[16,4096]{1,0:T(8,128)S(1)}, f32[16,32]{1,0:T(8,128)S(1)}) custom-call(bf16[64,4096]{1,0:T(8,128)(2,1)} %q_ref.1, bf16[32,128,1024]{2,1,0:T(8,128)(2,1)} %k_hbm.1, bf16[32,128,1024]{2,1,0:T(8,128)(2,1)} %v_hbm.1, s32[1,32]{1,0:T(1,128)} %lists.1, s32[1]{0:T(128)S(6)} %copy.11.counts), custom_call_target="tpu_custom_call" | custom-call | tf_op jit(solution)/shard_map/pallas_call | solution.py:296
  38.0 0.7 %copy.9 = f32[16,4096]{1,0:T(8,128)} copy(f32[16,4096]{1,0:T(8,128)S(1)} %get-tuple-element.2) | data formatting | bytes 524288
  38.7 0.6 %copy.10 = f32[16,32]{1,0:T(8,128)} copy(f32[16,32]{1,0:T(8,128)S(1)} %get-tuple-element.3) | data formatting | bytes 4096
where the time goes:
time: 39.5 us; the launch traced here: 39.3 us
  Pallas kernels  36.7 us (93%)
  local copies, waits for them, and re-layouts  1.3 us (3%)
  between operations  1.29 us (3%)
    pallas_call x1, Pallas kernels, on_device(): pl.pallas_call(functools.partial(kernel, plan), out_shape=(pltpu.VMEM((sh...  36.7 us
    unnamed x2, local copies, waits for them, and re-layouts  1.3 us

commit v1 on v0

v1 whole, which is shorter than its diff:
```python
import functools
import math

import jax
import jax.numpy as jnp
from jax import lax
from jax.experimental import pallas as pl
from jax.experimental.pallas import tpu as pltpu
from jax.sharding import PartitionSpec as P

DH = 128
PAGE = 128
LANES = 128
TILE = 256
ROWS = DH + 8
PAIR = 2
JOIN = 4
BLOCK = 16
PREFETCH = 2
SCALE = 1.0 / math.sqrt(DH)
LOG2_SCALE = SCALE * math.log2(math.e)

lowest = -1e30
highest = 3e38


def attend(query, k_ref, v_ref, caps, pages, acc, scores, turned):
    scaled = query * LOG2_SCALE
    high = scaled.astype(jnp.bfloat16)
    low = (scaled - high.astype(jnp.float32)).astype(jnp.bfloat16)
    turned[...] = jnp.concatenate([high, low], axis=1).T
    acc[...] = jnp.zeros_like(acc)
    ones = jnp.ones((16, PAIR * PAGE), jnp.bfloat16)
    block = min(BLOCK, pages)
    blocks = pages // block

    def score(index):
        rows = k_ref[index * block:(index + 1) * block].reshape(block * PAGE, DH)
        scores[index % 2] = jnp.dot(
            jnp.concatenate([rows, rows], axis=1), turned[...], preferred_element_type=jnp.float32
        ).reshape(block, PAGE, TILE)

    def weigh(index, at):
        page = index * block + at
        limits = [caps[page + i:page + i + 1, :] for i in range(PAIR)]
        top = functools.reduce(jnp.maximum, [
            jnp.minimum(jnp.max(scores[index % 2, at + i], axis=0, keepdims=True), limits[i]) for i in range(PAIR)
        ])
        weights = jnp.concatenate([
            jnp.exp2(scores[index % 2, at + i] - jnp.maximum(top, -limits[i])).astype(jnp.bfloat16)
            for i in range(PAIR)
        ], axis=0)
        left = jnp.concatenate([v_ref[page:page + PAIR].reshape(PAIR * PAGE, DH).T, ones], axis=0)
        return top, jnp.dot(left, weights, preferred_element_type=jnp.float32)[:ROWS]

    score(0)
    best = jnp.full((1, TILE), lowest, jnp.float32)
    for index in range(blocks):
        if index + 1 < blocks:
            score(index + 1)
        waiting = []
        for at in range(0, block, PAIR):
            waiting.append(weigh(index, at))
            if len(waiting) == JOIN or at + PAIR >= block:
                running = functools.reduce(jnp.maximum, [top for top, _ in waiting], best)
                joined = acc[...] * jnp.exp2(best - running)
                for top, out in waiting:
                    joined += out * jnp.exp2(top - running)
                acc[...] = joined
                best, waiting = running, []
    return best


def kernel(
    plan, q_hbm, k_hbm, v_hbm, lists_hbm, counts_hbm, out_ref, log_ref,
    lists, counts, caps, k_buf, v_buf, q_all, acc, scores, turned, part, part_in, cross_out, cross_in, piece_out, log_rows, log_out, log_in,
    lists_sem, counts_sem, k_sem, v_sem, own_sem, q_send, q_recv, pass_send, pass_recv,
    part_send, part_recv, cross_send, cross_recv, piece_send, piece_recv, log_send, log_recv,
):
    heads, tiles, sources, n_head, n_cache, cuts = plan
    batches = len(cuts) - 1
    groups = heads * tiles
    n_cross = n_cache // 2
    pages = k_hbm.shape[0]
    half = q_hbm.shape[0] // 2
    share = q_hbm.shape[0] // n_cache
    chunk = LANES // n_cross
    depth = DH // n_cross
    me = lax.axis_index("head")
    seat = lax.axis_index("cache")
    core = lax.rem(seat, 2)
    line = seat // 2
    sibling = seat + 1 - 2 * core

    def peer_of(index, count, offset):
        return lax.rem(index + offset, count)

    def load(head):
        columns = pl.ds(pl.multiple_of(head * DH, DH), DH)
        return (
            pltpu.make_async_copy(k_hbm.at[:, :, columns], k_buf.at[head], k_sem.at[head]),
            pltpu.make_async_copy(v_hbm.at[:, :, columns], v_buf.at[head], v_sem.at[head]),
        )

    def width_of(batch):
        return slice(cuts[batch] * DH, cuts[batch + 1] * DH)

    def query_source(batch, owner):
        rows = pl.ds(pl.multiple_of(core * half, half), half)
        start = pl.multiple_of((owner * heads + cuts[batch]) * DH, DH)
        return q_hbm.at[rows, pl.ds(start, (cuts[batch + 1] - cuts[batch]) * DH)]

    def own_query(batch):
        return pltpu.make_async_copy(
            query_source(batch, me), q_all.at[core, me, :, width_of(batch)], own_sem.at[batch]
        )

    def query_copy(batch, offset, source):
        peer = peer_of(me, n_head, offset)
        return pltpu.make_async_remote_copy(
            src_ref=query_source(batch, peer), dst_ref=q_all.at[core, source, :, width_of(batch)],
            send_sem=q_send.at[batch, offset - 1], recv_sem=q_recv.at[batch, source],
            device_id={"head": peer}, device_id_type=pl.DeviceIdType.MESH,
        )

    def pass_copy(batch, side):
        return pltpu.make_async_remote_copy(
            src_ref=q_all.at[side, :, :, width_of(batch)], dst_ref=q_all.at[side, :, :, width_of(batch)],
            send_sem=pass_send.at[batch], recv_sem=pass_recv.at[batch],
            device_id={"cache": sibling}, device_id_type=pl.DeviceIdType.MESH,
        )

    def part_copy(group):
        return pltpu.make_async_remote_copy(
            src_ref=part.at[group, 1 - core], dst_ref=part_in.at[group],
            send_sem=part_send.at[group], recv_sem=part_recv.at[group],
            device_id={"cache": sibling}, device_id_type=pl.DeviceIdType.MESH,
        )

    def cross_copy(group, offset, source):
        peer = peer_of(line, n_cross, offset)
        return pltpu.make_async_remote_copy(
            src_ref=cross_out.at[group, peer], dst_ref=cross_in.at[group, source],
            send_sem=cross_send.at[group, offset - 1], recv_sem=cross_recv.at[group, source],
            device_id={"cache": peer * 2 + core}, device_id_type=pl.DeviceIdType.MESH,
        )

    def columns_of(source, head):
        return pl.ds(pl.multiple_of((source * heads + head) * DH, DH), DH)

    def piece_copy(group, place, source, target):
        head = group // tiles
        return pltpu.make_async_remote_copy(
            src_ref=piece_out.at[group, place], dst_ref=out_ref.at[:, columns_of(source, head)],
            send_sem=piece_send.at[group, place], recv_sem=piece_recv.at[head, source],
            device_id={"head": target}, device_id_type=pl.DeviceIdType.MESH,
        )

    def log_copy(offset, source):
        peer = peer_of(me, n_head, offset)
        return pltpu.make_async_remote_copy(
            src_ref=log_out.at[peer], dst_ref=log_in.at[source],
            send_sem=log_send.at[offset - 1], recv_sem=log_recv.at[source],
            device_id={"head": peer}, device_id_type=pl.DeviceIdType.MESH,
        )

    barrier = pltpu.get_barrier_semaphore()
    for offset in range(1, n_head):
        pl.semaphore_signal(
            barrier, inc=1, device_id={"head": peer_of(me, n_head, offset)},
            device_id_type=pl.DeviceIdType.MESH,
        )
    pl.semaphore_signal(barrier, inc=1, device_id={"cache": sibling}, device_id_type=pl.DeviceIdType.MESH)
    for offset in range(1, n_cross):
        pl.semaphore_signal(
            barrier, inc=1, device_id={"cache": peer_of(line, n_cross, offset) * 2 + core},
            device_id_type=pl.DeviceIdType.MESH,
        )
    for batch in range(batches):
        own_query(batch).start()
    pl.semaphore_wait(barrier, n_head + n_cross - 1)
    for batch in range(batches):
        for offset in range(1, n_head):
            query_copy(batch, offset, me).start()
    lists_copy = pltpu.make_async_copy(lists_hbm, lists, lists_sem)
    counts_copy = pltpu.make_async_copy(counts_hbm, counts, counts_sem)
    lists_copy.start()
    counts_copy.start()
    for head in range(min(PREFETCH, heads)):
        for copy in load(head):
            copy.start()
    log_rows[...] = jnp.zeros_like(log_rows)
    lists_copy.wait()
    counts_copy.wait()
    slots = lists.shape[1]
    used = lax.broadcasted_iota(jnp.int32, (1, slots), 1) < counts[0]
    listed = jnp.where(used, lists[...], -1)
    match = listed == lax.broadcasted_iota(jnp.int32, (pages, slots), 0)
    cap = jnp.max(jnp.where(match, highest, lowest), axis=1, keepdims=True)
    caps[...] = jnp.broadcast_to(cap, caps.shape)

    def hand_on(batch):
        own_query(batch).wait()
        for offset in range(1, n_head):
            query_copy(batch, offset, peer_of(me, n_head, offset)).wait_recv()
        pass_copy(batch, core).start()

    def only_if(condition, action):
        if isinstance(condition, bool):
            if condition:
                action()
        else:
            pl.when(condition)(action)

    def compute(group):
        head = group // tiles
        tile = lax.rem(group, tiles)
        first = tiles == 1 or tile == 0

        def ready():
            for batch in range(batches):
                only_if(head == cuts[batch], lambda: pass_copy(batch, 1 - core).wait_recv())
            for copy in load(head):
                copy.wait()
            if heads > PREFETCH:
                @pl.when(head + PREFETCH < heads)
                def _():
                    for copy in load(head + PREFETCH):
                        copy.start()
            for batch in range(2, batches):
                pl.when(head == cuts[batch] - 1)(lambda: hand_on(batch))

        only_if(first, ready)
        members = [2 * x + side for side in range(2) for x in range(n_cross)]
        pieces = []
        for member in members:
            side, at = divmod(member * share, half)
            for l in range(sources):
                rows = q_all[side, tile * sources + l, :, pl.ds(pl.multiple_of(head * DH, DH), DH)]
                pieces.append(rows[at:at + share].astype(jnp.float32))
        query = jnp.concatenate(pieces, axis=0)

        best = attend(query, k_buf.at[head], v_buf.at[head], caps, pages, acc, scores, turned)
        row = lax.broadcasted_iota(jnp.int32, (8, TILE), 0)
        tail = jnp.where(row == 1, best, acc[DH:ROWS])
        for side in range(2):
            lanes = slice(side * LANES, (side + 1) * LANES)
            part[group, side, :DH] = acc[:DH, lanes]
            part[group, side, DH:ROWS] = tail[:, lanes]
        part_copy(group).start()

    def merge(group):
        part_copy(group).wait_recv()
        totals = [part[group, core, DH:DH + 1], part_in[group, DH:DH + 1]]
        bests = [part[group, core, DH + 1:DH + 2], part_in[group, DH + 1:DH + 2]]
        top = jnp.maximum(*bests)
        keeps = [jnp.exp2(best - top) for best in bests]
        total = totals[0] * keeps[0] + totals[1] * keeps[1]
        result = part[group, core, :DH] * keeps[0] + part_in[group, :DH] * keeps[1]
        row = lax.broadcasted_iota(jnp.int32, (8, LANES), 0)
        tail = jnp.where(row == 1, top, total)
        for x in range(n_cross):
            lanes = slice(x * chunk, (x + 1) * chunk)
            cross_out[group, x, :depth] = jnp.concatenate(
                [result[i * depth:(i + 1) * depth, lanes] for i in range(n_cross)], axis=1
            )
            cross_out[group, x, depth:] = jnp.concatenate([tail[:, lanes]] * n_cross, axis=1)
        for offset in range(1, n_cross):
            cross_copy(group, offset, line).start()
        cross_in[group, line] = cross_out[group, line]

    def finish(group):
        head = group // tiles
        tile = lax.rem(group, tiles)
        for offset in range(1, n_cross):
            cross_copy(group, offset, peer_of(line, n_cross, offset)).wait_recv()
        totals = [cross_in[group, x, depth:depth + 1] for x in range(n_cross)]
        bests = [cross_in[group, x, depth + 1:depth + 2] for x in range(n_cross)]
        top = functools.reduce(jnp.maximum, bests)
        keeps = [jnp.exp2(best - top) for best in bests]
        total = functools.reduce(jnp.add, [t * keep for t, keep in zip(totals, keeps)])
        inverse = 1.0 / total
        result = functools.reduce(
            jnp.add, [cross_in[group, x, :depth] * (keep * inverse) for x, keep in enumerate(keeps)]
        ).T
        log_rows[tile, pl.ds(me * heads + head, 1)] = top * math.log(2.0) + jnp.log(total)
        for l in range(sources):
            at = l * share
            piece_out[group, l] = jnp.concatenate(
                [result[i * chunk + at:i * chunk + at + share] for i in range(n_cross)], axis=1
            )
        send(group)

    def send(group):
        if tiles == 1:
            for offset in range(1, n_head):
                target = peer_of(me, n_head, offset)
                piece_copy(group, target, me, target).start()
            out_ref[:, columns_of(me, group)] = piece_out[group, me]
        else:
            for place in range(sources):
                target = lax.rem(group, tiles) * sources + place
                pl.when(target != me)(piece_copy(group, place, me, target).start)

                @pl.when(target == me)
                def _():
                    out_ref[:, columns_of(me, group // tiles)] = piece_out[group, place]

    def sent(group):
        if tiles == 1:
            for offset in range(1, n_head):
                target = peer_of(me, n_head, offset)
                piece_copy(group, target, me, target).wait_send()
        else:
            for place in range(sources):
                target = group % tiles * sources + place
                pl.when(target != me)(piece_copy(group, place, me, target).wait_send)

    for batch in range(min(2, batches)):
        hand_on(batch)

    def step(group, carry):
        compute(group)
        pl.when(group > 0)(lambda: merge(group - 1))
        pl.when(group > 2)(lambda: finish(group - 3))
        return carry

    lax.fori_loop(0, groups, step, 0)
    if groups > 2:
        finish(groups - 3)
    merge(groups - 1)
    for group in range(max(groups - 2, 0), groups):
        finish(group)
    for tile in range(tiles):
        columns = log_rows[tile].T
        for l in range(sources):
            log_out[tile * sources + l] = columns[l * share:(l + 1) * share]
    for offset in range(1, n_head):
        log_copy(offset, me).start()
    log_in[me] = log_out[me]
    for batch in range(batches):
        pass_copy(batch, core).wait_send()
        for offset in range(1, n_head):
            query_copy(batch, offset, me).wait_send()
    for group in range(groups):
        part_copy(group).wait_send()
        for offset in range(1, n_cross):
            cross_copy(group, offset, line).wait_send()
        sent(group)
    for head in range(heads):
        for offset in range(1, n_head):
            source = peer_of(me, n_head, offset)
            piece_copy(head * tiles, 0, source, source).wait_recv()
    for offset in range(1, n_head):
        log_copy(offset, me).wait_send()
    for offset in range(1, n_head):
        log_copy(offset, peer_of(me, n_head, offset)).wait_recv()
    log_ref[...] = functools.reduce(jnp.add, [log_in[s] for s in range(n_head)])[:, :log_ref.shape[1]]


def on_device(queries, keys, values, page_lists, page_counts):
    n_head = lax.axis_size("head")
    n_cache = lax.axis_size("cache")
    tok_local = queries.shape[0]
    heads = keys.shape[2] // DH
    pages = keys.shape[0]
    share = tok_local // n_cache
    sources = TILE // tok_local
    tiles = n_head // sources
    groups = heads * tiles
    n_cross = n_cache // 2
    depth = DH // n_cross
    cuts = tuple(sorted({0, min(1, heads), min(2, heads), min(4, heads), heads}))
    batches = len(cuts) - 1
    plan = (heads, tiles, sources, n_head, n_cache, cuts)
    dma = pltpu.SemaphoreType.DMA
    anywhere = pl.BlockSpec(memory_space=pl.ANY)
    attended, logged = pl.pallas_call(
        functools.partial(kernel, plan),
        out_shape=(
            pltpu.VMEM((share, queries.shape[1]), jnp.float32),
            pltpu.VMEM((share, n_head * heads), jnp.float32),
        ),
        in_specs=[anywhere] * 5,
        out_specs=(pl.BlockSpec(memory_space=pltpu.VMEM), pl.BlockSpec(memory_space=pltpu.VMEM)),
        scratch_shapes=[
            pltpu.VMEM(page_lists.shape, jnp.int32),
            pltpu.SMEM(page_counts.shape, jnp.int32),
            pltpu.VMEM((pages, TILE), jnp.float32),
            pltpu.VMEM((heads, pages, PAGE, DH), jnp.bfloat16),
            pltpu.VMEM((heads, pages, PAGE, DH), jnp.bfloat16),
            pltpu.VMEM((2, n_head, tok_local // 2, heads * DH), jnp.bfloat16),
            pltpu.VMEM((ROWS, TILE), jnp.float32),
            pltpu.VMEM((2, min(BLOCK, pages), PAGE, TILE), jnp.float32),
            pltpu.VMEM((2 * DH, TILE), jnp.bfloat16),
            pltpu.VMEM((groups, 2, ROWS, LANES), jnp.float32),
            pltpu.VMEM((groups, ROWS, LANES), jnp.float32),
            pltpu.VMEM((groups, n_cross, depth + 8, LANES), jnp.float32),
            pltpu.VMEM((groups, n_cross, depth + 8, LANES), jnp.float32),
            pltpu.VMEM((groups, sources, share, DH), jnp.float32),
            pltpu.VMEM((tiles, LANES, LANES), jnp.float32),
            pltpu.VMEM((n_head, share, LANES), jnp.float32),
            pltpu.VMEM((n_head, share, LANES), jnp.float32),
            dma(()),
            dma(()),
            dma((heads,)),
            dma((heads,)),
            dma((batches,)),
            dma((batches, n_head - 1)),
            dma((batches, n_head)),
            dma((batches,)),
            dma((batches,)),
            dma((groups,)),
            dma((groups,)),
            dma((groups, n_cross - 1)),
            dma((groups, n_cross)),
            dma((groups, sources)),
            dma((heads, n_head)),
            dma((n_head - 1,)),
            dma((n_head,)),
        ],
        compiler_params=pltpu.CompilerParams(
            collective_id=0, has_side_effects=True, vmem_limit_bytes=56 * 1024 * 1024
        ),
    )(queries, keys, values, page_lists, page_counts)
    return attended, logged


def solution(mesh):
    in_specs = (
        P(("group", "head"), None),
        P(("group", "cache"), None, "head"),
        P(("group", "cache"), None, "head"),
        P(("group", "cache"), None),
        P(("group", "cache")),
    )
    out_specs = (P(("group", "head", "cache"), None), P(("group", "head", "cache"), None))
    return jax.shard_map(
        on_device, mesh=mesh, in_specs=in_specs, out_specs=out_specs, check_vma=False
    )
```

time: 39.5 us -> 35.7 us (0.904)
  Pallas kernels: 36.7 us -> 32.9 us
    pallas_call x1, Pallas kernels: 36.7 us -> 32.9 us  [on_device(): pl.pallas_call(functools.partial(kernel, plan), out_shape=(pltpu.VMEM((sh...]
where the time goes in v1:
time: 35.7 us; the launch traced here: 35.5 us
  Pallas kernels  32.9 us (92%)
  local copies, waits for them, and re-layouts  1.3 us (4%)
  between operations  1.29 us (4%)
    pallas_call x1, Pallas kernels, on_device(): pl.pallas_call(functools.partial(kernel, plan), out_shape=(pltpu.VMEM((sh...  32.9 us
    unnamed x2, local copies, waits for them, and re-layouts  1.3 us

profile of v1, /device:TPU:0, one launch (start us, length us, event | category | flops | bytes accessed | tf_op | source)
XLA Modules:
  0.0 35.5 jit_solution(15970338280262741066)
XLA Ops:
  1.3 32.9 %shard_map.68 = (f32[16,4096]{1,0:T(8,128)S(1)}, f32[16,32]{1,0:T(8,128)S(1)}) custom-call(bf16[64,4096]{1,0:T(8,128)(2,1)} %q_hbm.1, bf16[32,128,1024]{2,1,0:T(8,128)(2,1)} %k_hbm.1, bf16[32,128,1024]{2,1,0:T(8,128)(2,1)} %v_hbm.1, s32[1,32]{1,0:T(1,128)} %lists_hbm.1, s32[1]{0:T(128)S(6)} %copy.11.counts_hbm), custom_call_target="tpu_custom_call" | custom-call | tf_op jit(solution)/shard_map/pallas_call | solution.py:378
  34.2 0.7 %copy.9 = f32[16,4096]{1,0:T(8,128)} copy(f32[16,4096]{1,0:T(8,128)S(1)} %get-tuple-element.2) | data formatting | bytes 524288
  34.9 0.6 %copy.10 = f32[16,32]{1,0:T(8,128)} copy(f32[16,32]{1,0:T(8,128)S(1)} %get-tuple-element.3) | data formatting | bytes 4096

commit v2 on v1

v2 whole, which is shorter than its diff:
```python
import functools
import math

import jax
import jax.numpy as jnp
from jax import lax
from jax.experimental import pallas as pl
from jax.experimental.pallas import tpu as pltpu
from jax.sharding import PartitionSpec as P

DH = 128
PAGE = 128
LANES = 128
TILE = 256
ROWS = DH + 8
PAIR = 2
JOIN = 4
BLOCK = 16
PREFETCH = 2
SCALE = 1.0 / math.sqrt(DH)
LOG2_E = math.log2(math.e)
LN_2 = math.log(2.0)
LOG2_SCALE = SCALE * LOG2_E

lowest = -1e30
highest = 3e38


def attend(query, k_ref, v_ref, caps, pages, acc, scores, turned):
    scaled = query * LOG2_SCALE
    high = scaled.astype(jnp.bfloat16)
    low = (scaled - high.astype(jnp.float32)).astype(jnp.bfloat16)
    turned[...] = jnp.concatenate([high, low], axis=1).T
    acc[...] = jnp.zeros_like(acc)
    ones = jnp.ones((16, PAIR * PAGE), jnp.bfloat16)
    block = min(BLOCK, pages)
    blocks = pages // block

    def score(index):
        rows = k_ref[index * block:(index + 1) * block].reshape(block * PAGE, DH)
        scores[index % 2] = jnp.dot(
            jnp.concatenate([rows, rows], axis=1), turned[...], preferred_element_type=jnp.float32
        ).reshape(block, PAGE, TILE)

    def weigh(index, at):
        page = index * block + at
        limits = [caps[page + i:page + i + 1, :] for i in range(PAIR)]
        top = functools.reduce(jnp.maximum, [
            jnp.minimum(jnp.max(scores[index % 2, at + i], axis=0, keepdims=True), limits[i]) for i in range(PAIR)
        ])
        weights = jnp.concatenate([
            jnp.exp2(scores[index % 2, at + i] - jnp.maximum(top, -limits[i])).astype(jnp.bfloat16)
            for i in range(PAIR)
        ], axis=0)
        left = jnp.concatenate([v_ref[page:page + PAIR].reshape(PAIR * PAGE, DH).T, ones], axis=0)
        return top, jnp.dot(left, weights, preferred_element_type=jnp.float32)[:ROWS]

    score(0)
    best = jnp.full((1, TILE), lowest, jnp.float32)
    for index in range(blocks):
        if index + 1 < blocks:
            score(index + 1)
        waiting = []
        for at in range(0, block, PAIR):
            waiting.append(weigh(index, at))
            if len(waiting) == JOIN or at + PAIR >= block:
                running = functools.reduce(jnp.maximum, [top for top, _ in waiting], best)
                joined = acc[...] * jnp.exp2(best - running)
                for top, out in waiting:
                    joined += out * jnp.exp2(top - running)
                acc[...] = joined
                best, waiting = running, []
    return best


def kernel(
    plan, q_hbm, k_hbm, v_hbm, lists_hbm, counts_hbm, out_ref, log_ref,
    lists, counts, caps, kv_buf, q_all, acc, scores, turned, part, part_in, piece_out, piece_in, log_out, log_in,
    lists_sem, counts_sem, kv_sem, own_sem, q_send, q_recv, pass_send, pass_recv,
    part_send, part_recv, piece_send, piece_recv, log_send, log_recv,
):
    heads, tiles, sources, n_head, n_cache, cuts = plan
    batches = len(cuts) - 1
    groups = heads * tiles
    n_cross = n_cache // 2
    others = n_head * n_cross - 1
    spots = n_cross * sources
    pages = k_hbm.shape[0]
    half = q_hbm.shape[0] // 2
    share = q_hbm.shape[0] // n_cache
    me = lax.axis_index("head")
    seat = lax.axis_index("cache")
    core = lax.rem(seat, 2)
    line = seat // 2
    sibling = seat + 1 - 2 * core
    place = line * n_head + me
    away = [(dx, dz) for dx in range(n_cross) for dz in range(n_head) if dx or dz]

    def peer_of(index, count, offset):
        return lax.rem(index + offset, count)

    def seat_of(x):
        return x * 2 + core

    def load(head):
        columns = pl.ds(pl.multiple_of(head * DH, DH), DH)
        sem = kv_sem.at[lax.rem(head, PREFETCH)]
        pltpu.make_async_copy(k_hbm.at[:, :, columns], kv_buf.at[head, 0], sem).start()
        pltpu.make_async_copy(v_hbm.at[:, :, columns], kv_buf.at[head, 1], sem).start()

    def wait_for(ref, sem):
        pltpu.make_async_copy(ref, ref, sem).wait()

    def width_of(batch):
        return slice(cuts[batch] * DH, cuts[batch + 1] * DH)

    def rows_of(batch, side):
        if batch == 0:
            return pl.ds(0, 2 * half)
        return pl.ds(pl.multiple_of(side * half, half), half)

    def query_source(first, last, owner):
        columns = pl.ds(pl.multiple_of((owner * heads + cuts[first]) * DH, DH), (cuts[last] - cuts[first]) * DH)
        return q_hbm.at[rows_of(first, core), columns]

    def own_copy(first, last):
        return pltpu.make_async_copy(
            query_source(first, last, me),
            q_all.at[me, rows_of(first, core), slice(cuts[first] * DH, cuts[last] * DH)], own_sem.at[min(first, 1)],
        )

    def send_queries(batch):
        for offset in range(1, n_head):
            peer = peer_of(me, n_head, offset)
            pltpu.make_async_remote_copy(
                src_ref=query_source(batch, batch + 1, peer),
                dst_ref=q_all.at[me, rows_of(batch, core), width_of(batch)],
                send_sem=q_send, recv_sem=q_recv.at[batch],
                device_id={"head": peer}, device_id_type=pl.DeviceIdType.MESH,
            ).start()

    def pass_copy(batch, side):
        return pltpu.make_async_remote_copy(
            src_ref=q_all.at[:, rows_of(batch, side), width_of(batch)],
            dst_ref=q_all.at[:, rows_of(batch, side), width_of(batch)],
            send_sem=pass_send, recv_sem=pass_recv.at[batch],
            device_id={"cache": sibling}, device_id_type=pl.DeviceIdType.MESH,
        )

    def arrive(batch):
        wait_for(q_all.at[pl.ds(0, n_head - 1), rows_of(batch, 0), width_of(batch)], q_recv.at[batch])

    def hand_on(batch):
        arrive(batch)
        pass_copy(batch, core).start()

    def part_copy(group):
        return pltpu.make_async_remote_copy(
            src_ref=part.at[group, 1 - core], dst_ref=part_in.at[group],
            send_sem=part_send, recv_sem=part_recv.at[group],
            device_id={"cache": sibling}, device_id_type=pl.DeviceIdType.MESH,
        )

    def piece_copy(group, x, z):
        return pltpu.make_async_remote_copy(
            src_ref=piece_out.at[group, x, lax.rem(z, sources)], dst_ref=piece_in.at[place, group // tiles],
            send_sem=piece_send, recv_sem=piece_recv,
            device_id={"head": z, "cache": seat_of(x)}, device_id_type=pl.DeviceIdType.MESH,
        )

    barrier = pltpu.get_barrier_semaphore()
    for dx, dz in away:
        pl.semaphore_signal(
            barrier, inc=1,
            device_id={"head": peer_of(me, n_head, dz), "cache": seat_of(peer_of(line, n_cross, dx))},
            device_id_type=pl.DeviceIdType.MESH,
        )
    pl.semaphore_signal(barrier, inc=1, device_id={"cache": sibling}, device_id_type=pl.DeviceIdType.MESH)
    own_copies = [own_copy(0, 1)] + ([own_copy(1, batches)] if batches > 1 else [])
    for copy in own_copies:
        copy.start()
    lists_copy = pltpu.make_async_copy(lists_hbm, lists, lists_sem)
    counts_copy = pltpu.make_async_copy(counts_hbm, counts, counts_sem)
    lists_copy.start()
    counts_copy.start()
    pl.semaphore_wait(barrier, others + 1)
    for batch in range(min(3, batches)):
        send_queries(batch)
    load(0)
    log_out[...] = jnp.zeros_like(log_out)
    lists_copy.wait()
    counts_copy.wait()
    slots = lists.shape[1]
    used = lax.broadcasted_iota(jnp.int32, (1, slots), 1) < counts[0]
    listed = jnp.where(used, lists[...], -1)
    match = listed == lax.broadcasted_iota(jnp.int32, (pages, slots), 0)
    cap = jnp.max(jnp.where(match, highest, lowest), axis=1, keepdims=True)
    caps[...] = jnp.broadcast_to(cap, caps.shape)
    for copy in own_copies:
        copy.wait()
    for head in range(1, min(PREFETCH, heads)):
        load(head)
    arrive(0)
    for batch in range(3, batches):
        send_queries(batch)
    if batches > 1:
        hand_on(1)

    def only_if(condition, action):
        if isinstance(condition, bool):
            if condition:
                action()
        else:
            pl.when(condition)(action)

    def compute(group):
        head = group // tiles
        tile = lax.rem(group, tiles)

        def ready():
            for batch in range(1, batches):
                pl.when(head == cuts[batch])(lambda: pass_copy(batch, 1 - core).wait_recv())
            wait_for(kv_buf.at[head], kv_sem.at[lax.rem(head, PREFETCH)])
            if heads > PREFETCH:
                pl.when(head + PREFETCH < heads)(lambda: load(head + PREFETCH))
            for batch in range(2, batches):
                pl.when(head == cuts[batch] - 1)(lambda: hand_on(batch))

        only_if(tiles == 1 or tile == 0, ready)
        members = [2 * x + side for side in range(2) for x in range(n_cross)]
        pieces = []
        for member in members:
            for l in range(sources):
                rows = q_all[tile * sources + l, :, pl.ds(pl.multiple_of(head * DH, DH), DH)]
                pieces.append(rows[member * share:(member + 1) * share].astype(jnp.float32))
        query = jnp.concatenate(pieces, axis=0)
        best = attend(query, kv_buf.at[head, 0], kv_buf.at[head, 1], caps, pages, acc, scores, turned)
        row = lax.broadcasted_iota(jnp.int32, (8, TILE), 0)
        tail = jnp.where(row == 1, best, acc[DH:ROWS])
        for side in range(2):
            lanes = slice(side * LANES, (side + 1) * LANES)
            part[group, side, :DH] = acc[:DH, lanes]
            part[group, side, DH:ROWS] = tail[:, lanes]
        part_copy(group).start()

    def merge(group):
        head = group // tiles
        tile = lax.rem(group, tiles)
        part_copy(group).wait_recv()
        totals = [part[group, core, DH:DH + 1], part_in[group, DH:DH + 1]]
        bests = [part[group, core, DH + 1:DH + 2], part_in[group, DH + 1:DH + 2]]
        top = jnp.maximum(*bests)
        keeps = [jnp.exp2(best - top) for best in bests]
        total = totals[0] * keeps[0] + totals[1] * keeps[1]
        inverse = 1.0 / total
        result = part[group, core, :DH] * (keeps[0] * inverse) + part_in[group, :DH] * (keeps[1] * inverse)
        level = jnp.broadcast_to(top + jnp.log(total) * LOG2_E, (spots, LANES))
        level = pltpu.roll(level, 0, 1, stride=share, stride_axis=0)
        level = pltpu.roll(level, lax.rem((head + 1) * share, LANES), 1)
        lane = lax.broadcasted_iota(jnp.int32, (spots, LANES), 1)
        chosen = jnp.logical_and(lane >= head * share, lane < (head + 1) * share)
        log_out[tile] = jnp.where(chosen, level, log_out[tile])
        rows = result.T
        for x in range(n_cross):
            for l in range(sources):
                at = (x * sources + l) * share
                piece_out[group, x, l] = rows[at:at + share]
        if tiles == 1:
            for dx, dz in away:
                piece_copy(group, peer_of(line, n_cross, dx), peer_of(me, n_head, dz)).start()
            piece_in[place, head] = piece_out[group, line, me]
        else:
            for dx in range(n_cross):
                x = peer_of(line, n_cross, dx)
                for l in range(sources):
                    z = tile * sources + l
                    if dx:
                        piece_copy(group, x, z).start()
                    else:
                        pl.when(z != me)(piece_copy(group, x, z).start)

                        @pl.when(z == me)
                        def _():
                            piece_in[place, head] = piece_out[group, line, l]

    def step(group, carry):
        compute(group)
        pl.when(group > 0)(lambda: merge(group - 1))
        return carry

    lax.fori_loop(0, groups, step, 0)
    merge(groups - 1)
    for dx, dz in away:
        x, z = peer_of(line, n_cross, dx), peer_of(me, n_head, dz)
        pltpu.make_async_remote_copy(
            src_ref=log_out.at[z // sources, pl.ds(spots - 1 - x * sources - lax.rem(z, sources), 1)],
            dst_ref=log_in.at[pl.ds(place, 1)], send_sem=log_send, recv_sem=log_recv,
            device_id={"head": z, "cache": seat_of(x)}, device_id_type=pl.DeviceIdType.MESH,
        ).start()
    log_in[pl.ds(place, 1)] = log_out[me // sources, pl.ds(spots - 1 - line * sources - lax.rem(me, sources), 1)]
    wait_for(q_all.at[pl.ds(0, n_head - 1), :, width_of(0)], q_send)
    if batches > 1:
        rest = slice(cuts[1] * DH, heads * DH)
        wait_for(q_all.at[pl.ds(0, n_head - 1), rows_of(1, core), rest], q_send)
        wait_for(q_all.at[:, rows_of(1, core), rest], pass_send)
    wait_for(part.at[:, 0], part_send)
    wait_for(piece_in.at[pl.ds(0, others)], piece_send)
    wait_for(piece_in.at[pl.ds(0, others)], piece_recv)
    wait_for(log_in.at[pl.ds(0, others)], log_send)
    wait_for(log_in.at[pl.ds(0, others)], log_recv)
    levels = [log_in[x * n_head:(x + 1) * n_head] for x in range(n_cross)]
    top = functools.reduce(jnp.maximum, levels)
    keeps = [jnp.exp2(level - top) for level in levels]
    total = functools.reduce(jnp.add, keeps)
    inverse = 1.0 / total
    columns = [(keep * inverse).T for keep in keeps]
    logged = (top * LN_2 + jnp.log(total)).T
    lane = lax.broadcasted_iota(jnp.int32, log_ref.shape, 1)
    logs = jnp.zeros(log_ref.shape, jnp.float32)
    for z in range(n_head):
        for head in range(heads):
            column = z * heads + head
            rows = slice(head * share, (head + 1) * share)
            out_ref[:, column * DH:(column + 1) * DH] = functools.reduce(jnp.add, [
                piece_in[x * n_head + z, head] * columns[x][rows, z:z + 1] for x in range(n_cross)
            ])
            logs = jnp.where(lane == column, logged[rows, z:z + 1], logs)
    log_ref[...] = logs


def on_device(queries, keys, values, page_lists, page_counts):
    n_head = lax.axis_size("head")
    n_cache = lax.axis_size("cache")
    tok_local = queries.shape[0]
    heads = keys.shape[2] // DH
    pages = keys.shape[0]
    share = tok_local // n_cache
    sources = TILE // tok_local
    tiles = n_head // sources
    groups = heads * tiles
    n_cross = n_cache // 2
    cuts = tuple(sorted({0, min(1, heads), min(2, heads), min(4, heads), heads}))
    batches = len(cuts) - 1
    plan = (heads, tiles, sources, n_head, n_cache, cuts)
    dma = pltpu.SemaphoreType.DMA
    anywhere = pl.BlockSpec(memory_space=pl.ANY)
    attended, logged = pl.pallas_call(
        functools.partial(kernel, plan),
        out_shape=(
            pltpu.VMEM((share, queries.shape[1]), jnp.float32),
            pltpu.VMEM((share, n_head * heads), jnp.float32),
        ),
        in_specs=[anywhere] * 5,
        out_specs=(pl.BlockSpec(memory_space=pltpu.VMEM), pl.BlockSpec(memory_space=pltpu.VMEM)),
        scratch_shapes=[
            pltpu.VMEM(page_lists.shape, jnp.int32),
            pltpu.SMEM(page_counts.shape, jnp.int32),
            pltpu.VMEM((pages, TILE), jnp.float32),
            pltpu.VMEM((heads, 2, pages, PAGE, DH), jnp.bfloat16),
            pltpu.VMEM((n_head, tok_local, heads * DH), jnp.bfloat16),
            pltpu.VMEM((ROWS, TILE), jnp.float32),
            pltpu.VMEM((2, min(BLOCK, pages), PAGE, TILE), jnp.float32),
            pltpu.VMEM((2 * DH, TILE), jnp.bfloat16),
            pltpu.VMEM((groups, 2, ROWS, LANES), jnp.float32),
            pltpu.VMEM((groups, ROWS, LANES), jnp.float32),
            pltpu.VMEM((groups, n_cross, sources, share, DH), jnp.float32),
            pltpu.VMEM((n_cross * n_head, heads, share, DH), jnp.float32),
            pltpu.VMEM((tiles, n_cross * sources, LANES), jnp.float32),
            pltpu.VMEM((n_cross * n_head, LANES), jnp.float32),
            dma(()),
            dma(()),
            dma((PREFETCH,)),
            dma((2,)),
            dma(()),
            dma((batches,)),
            dma(()),
            dma((batches,)),
            dma(()),
            dma((groups,)),
            dma(()),
            dma(()),
            dma(()),
            dma(()),
        ],
        compiler_params=pltpu.CompilerParams(
            collective_id=0, has_side_effects=True, vmem_limit_bytes=56 * 1024 * 1024
        ),
    )(queries, keys, values, page_lists, page_counts)
    return attended, logged


def solution(mesh):
    in_specs = (
        P(("group", "head"), None),
        P(("group", "cache"), None, "head"),
        P(("group", "cache"), None, "head"),
        P(("group", "cache"), None),
        P(("group", "cache")),
    )
    out_specs = (P(("group", "head", "cache"), None), P(("group", "head", "cache"), None))
    return jax.shard_map(
        on_device, mesh=mesh, in_specs=in_specs, out_specs=out_specs, check_vma=False
    )
```

time: 35.7 us -> 31.4 us (0.88)
  Pallas kernels: 32.9 us -> 28.7 us
    pallas_call x1, Pallas kernels: 32.9 us -> 28.7 us  [on_device(): pl.pallas_call(functools.partial(kernel, plan), out_shape=(pltpu.VMEM((sh...]
where the time goes in v2:
time: 31.4 us; the launch traced here: 31.3 us
  Pallas kernels  28.7 us (91%)
  local copies, waits for them, and re-layouts  1.3 us (4%)
  between operations  1.29 us (4%)
    pallas_call x1, Pallas kernels, on_device(): pl.pallas_call(functools.partial(kernel, plan), out_shape=(pltpu.VMEM((sh...  28.7 us
    unnamed x2, local copies, waits for them, and re-layouts  1.3 us

profile of v2, /device:TPU:0, one launch (start us, length us, event | category | flops | bytes accessed | tf_op | source)
XLA Modules:
  0.0 31.3 jit_solution(16928930106026400671)
XLA Ops:
  1.3 28.7 %shard_map.68 = (f32[16,4096]{1,0:T(8,128)S(1)}, f32[16,32]{1,0:T(8,128)S(1)}) custom-call(bf16[64,4096]{1,0:T(8,128)(2,1)} %q_hbm.1, bf16[32,128,1024]{2,1,0:T(8,128)(2,1)} %k_hbm.1, bf16[32,128,1024]{2,1,0:T(8,128)(2,1)} %v_hbm.1, s32[1,32]{1,0:T(1,128)} %lists_hbm.1, s32[1]{0:T(128)S(6)} %copy.11.counts_hbm), custom_call_target="tpu_custom_call" | custom-call | tf_op jit(solution)/shard_map/pallas_call | solution.py:347
  30.0 0.7 %copy.9 = f32[16,4096]{1,0:T(8,128)} copy(f32[16,4096]{1,0:T(8,128)S(1)} %get-tuple-element.2) | data formatting | bytes 524288
  30.7 0.6 %copy.10 = f32[16,32]{1,0:T(8,128)} copy(f32[16,32]{1,0:T(8,128)S(1)} %get-tuple-element.3) | data formatting | bytes 4096

commit v3 on v2

--- a/solution.py
+++ b/solution.py
@@ -326,6 +326,17 @@
             ])
             logs = jnp.where(lane == column, logged[rows, z:z + 1], logs)
     log_ref[...] = logs
+
+
+def store(attended, logged, attended_hbm, logged_hbm, attended_sem, logged_sem):
+    copies = (
+        pltpu.make_async_copy(attended, attended_hbm, attended_sem),
+        pltpu.make_async_copy(logged, logged_hbm, logged_sem),
+    )
+    for copy in copies:
+        copy.start()
+    for copy in copies:
+        copy.wait()
 
 
 def on_device(queries, keys, values, page_lists, page_counts):
@@ -386,7 +397,15 @@
             collective_id=0, has_side_effects=True, vmem_limit_bytes=56 * 1024 * 1024
         ),
     )(queries, keys, values, page_lists, page_counts)
-    return attended, logged
+    return pl.pallas_call(
+        store,
+        out_shape=(
+            jax.ShapeDtypeStruct(attended.shape, jnp.float32), jax.ShapeDtypeStruct(logged.shape, jnp.float32)
+        ),
+        in_specs=[pl.BlockSpec(memory_space=pltpu.VMEM)] * 2,
+        out_specs=(anywhere, anywhere),
+        scratch_shapes=[dma(()), dma(())],
+    )(pltpu.with_memory_space_constraint(attended, pltpu.VMEM), pltpu.with_memory_space_constraint(logged, pltpu.VMEM))
 
 
 def solution(mesh):

time: 31.4 us -> 30.8 us (0.981)
  local copies, waits for them, and re-layouts: 1.3 us -> 0 us
  Pallas kernels: 28.7 us -> 29.4 us
    unnamed x2 -> x0, local copies, waits for them, and re-layouts: 1.3 us -> none
    pallas_call x0 -> x1, Pallas kernels: none -> 0.72 us  [on_device(): pl.pallas_call(store, out_shape=(jax.ShapeDtypeStruct(attended.shape, jnp...]
where the time goes in v3:
time: 30.8 us; the launch traced here: 30.7 us
  Pallas kernels  29.4 us (95%)
  between operations  1.29 us (4%)
    pallas_call x1, Pallas kernels, on_device(): pl.pallas_call(functools.partial(kernel, plan), out_shape=(pltpu.VMEM((sh...  28.7 us
    pallas_call x1, Pallas kernels, on_device(): pl.pallas_call(store, out_shape=(jax.ShapeDtypeStruct(attended.shape, jnp...  0.72 us

profile of v3, /device:TPU:0, one launch (start us, length us, event | category | flops | bytes accessed | tf_op | source)
XLA Modules:
  0.0 30.7 jit_solution(12939038321993776260)
XLA Ops:
  1.3 28.7 %shard_map.68 = (f32[16,4096]{1,0:T(8,128)S(1)}, f32[16,32]{1,0:T(8,128)S(1)}) custom-call(bf16[64,4096]{1,0:T(8,128)(2,1)} %q_hbm.1, bf16[32,128,1024]{2,1,0:T(8,128)(2,1)} %k_hbm.1, bf16[32,128,1024]{2,1,0:T(8,128)(2,1)} %v_hbm.1, s32[1,32]{1,0:T(1,128)} %lists_hbm.1, s32[1]{0:T(128)S(6)} %copy.7.counts_hbm), custom_call_target="tpu_custom_call" | custom-call | tf_op jit(solution)/shard_map/pallas_call | solution.py:358
  30.0 0.7 %shard_map.69 = (f32[16,4096]{1,0:T(8,128)}, f32[16,32]{1,0:T(8,128)}) custom-call(f32[16,4096]{1,0:T(8,128)S(1)} %get-tuple-element.4.attended, f32[16,32]{1,0:T(8,128)S(1)} %get-tuple-element.5.logged), custom_call_target="tpu_custom_call" | custom-call | tf_op jit(solution)/shard_map/pallas_call | solution.py:400

commit v4 on v3

--- a/solution.py
+++ b/solution.py
@@ -15,7 +15,6 @@
 ROWS = DH + 8
 PAIR = 2
 JOIN = 4
-BLOCK = 16
 PREFETCH = 2
 SCALE = 1.0 / math.sqrt(DH)
 LOG2_E = math.log2(math.e)
@@ -31,51 +30,50 @@
     high = scaled.astype(jnp.bfloat16)
     low = (scaled - high.astype(jnp.float32)).astype(jnp.bfloat16)
     turned[...] = jnp.concatenate([high, low], axis=1).T
-    acc[...] = jnp.zeros_like(acc)
     ones = jnp.ones((16, PAIR * PAGE), jnp.bfloat16)
-    block = min(BLOCK, pages)
-    blocks = pages // block
-
-    def score(index):
-        rows = k_ref[index * block:(index + 1) * block].reshape(block * PAGE, DH)
-        scores[index % 2] = jnp.dot(
+    cut = pages * 3 // 16 * 2
+    blocks = [(0, cut), (cut, pages)]
+
+    def score(first, last):
+        rows = k_ref[first:last].reshape((last - first) * PAGE, DH)
+        scores[first:last] = jnp.dot(
             jnp.concatenate([rows, rows], axis=1), turned[...], preferred_element_type=jnp.float32
-        ).reshape(block, PAGE, TILE)
-
-    def weigh(index, at):
-        page = index * block + at
+        ).reshape(last - first, PAGE, TILE)
+
+    def weigh(page):
         limits = [caps[page + i:page + i + 1, :] for i in range(PAIR)]
         top = functools.reduce(jnp.maximum, [
-            jnp.minimum(jnp.max(scores[index % 2, at + i], axis=0, keepdims=True), limits[i]) for i in range(PAIR)
+            jnp.minimum(jnp.max(scores[page + i], axis=0, keepdims=True), limits[i]) for i in range(PAIR)
         ])
         weights = jnp.concatenate([
-            jnp.exp2(scores[index % 2, at + i] - jnp.maximum(top, -limits[i])).astype(jnp.bfloat16)
-            for i in range(PAIR)
+            jnp.exp2(scores[page + i] - jnp.maximum(top, -limits[i])).astype(jnp.bfloat16) for i in range(PAIR)
         ], axis=0)
         left = jnp.concatenate([v_ref[page:page + PAIR].reshape(PAIR * PAGE, DH).T, ones], axis=0)
         return top, jnp.dot(left, weights, preferred_element_type=jnp.float32)[:ROWS]
 
-    score(0)
+    score(*blocks[0])
     best = jnp.full((1, TILE), lowest, jnp.float32)
-    for index in range(blocks):
-        if index + 1 < blocks:
-            score(index + 1)
+    started = False
+    for index, (first, last) in enumerate(blocks):
+        if index + 1 < len(blocks):
+            score(*blocks[index + 1])
         waiting = []
-        for at in range(0, block, PAIR):
-            waiting.append(weigh(index, at))
-            if len(waiting) == JOIN or at + PAIR >= block:
+        for page in range(first, last, PAIR):
+            waiting.append(weigh(page))
+            if len(waiting) == JOIN or page + PAIR >= last:
                 running = functools.reduce(jnp.maximum, [top for top, _ in waiting], best)
-                joined = acc[...] * jnp.exp2(best - running)
-                for top, out in waiting:
-                    joined += out * jnp.exp2(top - running)
-                acc[...] = joined
-                best, waiting = running, []
+                joined = functools.reduce(jnp.add, [out * jnp.exp2(top - running) for top, out in waiting])
+                if started:
+                    joined += jnp.concatenate([acc[0], acc[1]], axis=1) * jnp.exp2(best - running)
+                acc[0] = joined[:, :LANES]
+                acc[1] = joined[:, LANES:]
+                best, waiting, started = running, [], True
     return best
 
 
 def kernel(
     plan, q_hbm, k_hbm, v_hbm, lists_hbm, counts_hbm, out_ref, log_ref,
-    lists, counts, caps, kv_buf, q_all, acc, scores, turned, part, part_in, piece_out, piece_in, log_out, log_in,
+    lists, counts, caps, kv_buf, q_all, scores, turned, part, part_in, piece_out, piece_in, log_out, log_in,
     lists_sem, counts_sem, kv_sem, own_sem, q_send, q_recv, pass_send, pass_recv,
     part_send, part_recv, piece_send, piece_recv, log_send, log_recv,
 ):
@@ -94,10 +92,14 @@
     line = seat // 2
     sibling = seat + 1 - 2 * core
     place = line * n_head + me
-    away = [(dx, dz) for dx in range(n_cross) for dz in range(n_head) if dx or dz]
+    upper = me // (n_head // 2)
+    away = [(dx, dz) for dz in [*range(1, n_head), 0] for dx in reversed(range(n_cross)) if dx or dz]
 
     def peer_of(index, count, offset):
         return lax.rem(index + offset, count)
+
+    def far_first(rank):
+        return lax.rem(me + n_head - rank + upper * (2 * rank - n_head) + n_head, n_head) if rank else me
 
     def seat_of(x):
         return x * 2 + core
@@ -130,8 +132,8 @@
         )
 
     def send_queries(batch):
-        for offset in range(1, n_head):
-            peer = peer_of(me, n_head, offset)
+        for rank in range(1, n_head):
+            peer = far_first(rank)
             pltpu.make_async_remote_copy(
                 src_ref=query_source(batch, batch + 1, peer),
                 dst_ref=q_all.at[me, rows_of(batch, core), width_of(batch)],
@@ -172,7 +174,7 @@
     for dx, dz in away:
         pl.semaphore_signal(
             barrier, inc=1,
-            device_id={"head": peer_of(me, n_head, dz), "cache": seat_of(peer_of(line, n_cross, dx))},
+            device_id={"head": far_first(dz), "cache": seat_of(peer_of(line, n_cross, dx))},
             device_id_type=pl.DeviceIdType.MESH,
         )
     pl.semaphore_signal(barrier, inc=1, device_id={"cache": sibling}, device_id_type=pl.DeviceIdType.MESH)
@@ -234,13 +236,9 @@
                 rows = q_all[tile * sources + l, :, pl.ds(pl.multiple_of(head * DH, DH), DH)]
                 pieces.append(rows[member * share:(member + 1) * share].astype(jnp.float32))
         query = jnp.concatenate(pieces, axis=0)
-        best = attend(query, kv_buf.at[head, 0], kv_buf.at[head, 1], caps, pages, acc, scores, turned)
-        row = lax.broadcasted_iota(jnp.int32, (8, TILE), 0)
-        tail = jnp.where(row == 1, best, acc[DH:ROWS])
+        best = attend(query, kv_buf.at[head, 0], kv_buf.at[head, 1], caps, pages, part.at[group], scores, turned)
         for side in range(2):
-            lanes = slice(side * LANES, (side + 1) * LANES)
-            part[group, side, :DH] = acc[:DH, lanes]
-            part[group, side, DH:ROWS] = tail[:, lanes]
+            part[group, side, DH + 1:DH + 2] = best[:, side * LANES:(side + 1) * LANES]
         part_copy(group).start()
 
     def merge(group):
@@ -267,7 +265,7 @@
                 piece_out[group, x, l] = rows[at:at + share]
         if tiles == 1:
             for dx, dz in away:
-                piece_copy(group, peer_of(line, n_cross, dx), peer_of(me, n_head, dz)).start()
+                piece_copy(group, peer_of(line, n_cross, dx), far_first(dz)).start()
             piece_in[place, head] = piece_out[group, line, me]
         else:
             for dx in range(n_cross):
@@ -291,7 +289,7 @@
     lax.fori_loop(0, groups, step, 0)
     merge(groups - 1)
     for dx, dz in away:
-        x, z = peer_of(line, n_cross, dx), peer_of(me, n_head, dz)
+        x, z = peer_of(line, n_cross, dx), far_first(dz)
         pltpu.make_async_remote_copy(
             src_ref=log_out.at[z // sources, pl.ds(spots - 1 - x * sources - lax.rem(z, sources), 1)],
             dst_ref=log_in.at[pl.ds(place, 1)], send_sem=log_send, recv_sem=log_recv,
@@ -369,8 +367,7 @@
             pltpu.VMEM((pages, TILE), jnp.float32),
             pltpu.VMEM((heads, 2, pages, PAGE, DH), jnp.bfloat16),
             pltpu.VMEM((n_head, tok_local, heads * DH), jnp.bfloat16),
-            pltpu.VMEM((ROWS, TILE), jnp.float32),
-            pltpu.VMEM((2, min(BLOCK, pages), PAGE, TILE), jnp.float32),
+            pltpu.VMEM((pages, PAGE, TILE), jnp.float32),
             pltpu.VMEM((2 * DH, TILE), jnp.bfloat16),
             pltpu.VMEM((groups, 2, ROWS, LANES), jnp.float32),
             pltpu.VMEM((groups, ROWS, LANES), jnp.float32),

time: 30.8 us -> 30.3 us (0.984)
  Pallas kernels: 29.4 us -> 28.9 us
    pallas_call x1, Pallas kernels: 28.7 us -> 28.1 us  [on_device(): pl.pallas_call(functools.partial(kernel, plan), out_shape=(pltpu.VMEM((sh...]
where the time goes in v4:
time: 30.3 us; the launch traced here: 30.1 us
  Pallas kernels  28.9 us (95%)
  between operations  1.29 us (4%)
    pallas_call x1, Pallas kernels, on_device(): pl.pallas_call(functools.partial(kernel, plan), out_shape=(pltpu.VMEM((sh...  28.1 us
    pallas_call x1, Pallas kernels, on_device(): pl.pallas_call(store, out_shape=(jax.ShapeDtypeStruct(attended.shape, jnp...  0.72 us

profile of v4, /device:TPU:0, one launch (start us, length us, event | category | flops | bytes accessed | tf_op | source)
XLA Modules:
  0.0 30.1 jit_solution(15681816917054470167)
XLA Ops:
  1.3 28.1 %shard_map.68 = (f32[16,4096]{1,0:T(8,128)S(1)}, f32[16,32]{1,0:T(8,128)S(1)}) custom-call(bf16[64,4096]{1,0:T(8,128)(2,1)} %q_hbm.1, bf16[32,128,1024]{2,1,0:T(8,128)(2,1)} %k_hbm.1, bf16[32,128,1024]{2,1,0:T(8,128)(2,1)} %v_hbm.1, s32[1,32]{1,0:T(1,128)} %lists_hbm.1, s32[1]{0:T(128)S(6)} %copy.7.counts_hbm), custom_call_target="tpu_custom_call" | custom-call | tf_op jit(solution)/shard_map/pallas_call | solution.py:356
  29.4 0.7 %shard_map.69 = (f32[16,4096]{1,0:T(8,128)}, f32[16,32]{1,0:T(8,128)}) custom-call(f32[16,4096]{1,0:T(8,128)S(1)} %get-tuple-element.4.attended, f32[16,32]{1,0:T(8,128)S(1)} %get-tuple-element.5.logged), custom_call_target="tpu_custom_call" | custom-call | tf_op jit(solution)/shard_map/pallas_call | solution.py:397

commit v5 on v4

--- a/solution.py
+++ b/solution.py
@@ -14,7 +14,7 @@
 TILE = 256
 ROWS = DH + 8
 PAIR = 2
-JOIN = 4
+JOIN = 8
 PREFETCH = 2
 SCALE = 1.0 / math.sqrt(DH)
 LOG2_E = math.log2(math.e)
@@ -72,8 +72,8 @@
 
 
 def kernel(
-    plan, q_hbm, k_hbm, v_hbm, lists_hbm, counts_hbm, out_ref, log_ref,
-    lists, counts, caps, kv_buf, q_all, scores, turned, part, part_in, piece_out, piece_in, log_out, log_in,
+    plan, q_hbm, k_hbm, v_hbm, lists_hbm, counts_hbm, piece_in, log_in,
+    lists, counts, caps, kv_buf, q_all, scores, turned, part, part_in, piece_out, log_out,
     lists_sem, counts_sem, kv_sem, own_sem, q_send, q_recv, pass_send, pass_recv,
     part_send, part_recv, piece_send, piece_recv, log_send, log_recv,
 ):
@@ -306,35 +306,40 @@
     wait_for(piece_in.at[pl.ds(0, others)], piece_recv)
     wait_for(log_in.at[pl.ds(0, others)], log_send)
     wait_for(log_in.at[pl.ds(0, others)], log_recv)
+
+
+def combine(plan, piece_in, log_in, attended_hbm, logged_hbm, attended, logged, attended_sem, logged_sem):
+    heads, _, _, n_head, n_cache, _ = plan
+    n_cross = n_cache // 2
+    share = attended.shape[0]
+    width = heads * DH
     levels = [log_in[x * n_head:(x + 1) * n_head] for x in range(n_cross)]
     top = functools.reduce(jnp.maximum, levels)
     keeps = [jnp.exp2(level - top) for level in levels]
     total = functools.reduce(jnp.add, keeps)
     inverse = 1.0 / total
     columns = [(keep * inverse).T for keep in keeps]
-    logged = (top * LN_2 + jnp.log(total)).T
-    lane = lax.broadcasted_iota(jnp.int32, log_ref.shape, 1)
-    logs = jnp.zeros(log_ref.shape, jnp.float32)
+    values = (top * LN_2 + jnp.log(total)).T
+    lane = lax.broadcasted_iota(jnp.int32, logged.shape, 1)
+    logs = jnp.zeros(logged.shape, jnp.float32)
     for z in range(n_head):
         for head in range(heads):
-            column = z * heads + head
             rows = slice(head * share, (head + 1) * share)
-            out_ref[:, column * DH:(column + 1) * DH] = functools.reduce(jnp.add, [
+            logs = jnp.where(lane == z * heads + head, values[rows, z:z + 1], logs)
+    logged[...] = logs
+    logged_copy = pltpu.make_async_copy(logged, logged_hbm, logged_sem)
+    logged_copy.start()
+    for z in range(n_head):
+        for head in range(heads):
+            at = z * width + head * DH
+            rows = slice(head * share, (head + 1) * share)
+            attended[:, at:at + DH] = functools.reduce(jnp.add, [
                 piece_in[x * n_head + z, head] * columns[x][rows, z:z + 1] for x in range(n_cross)
             ])
-            logs = jnp.where(lane == column, logged[rows, z:z + 1], logs)
-    log_ref[...] = logs
-
-
-def store(attended, logged, attended_hbm, logged_hbm, attended_sem, logged_sem):
-    copies = (
-        pltpu.make_async_copy(attended, attended_hbm, attended_sem),
-        pltpu.make_async_copy(logged, logged_hbm, logged_sem),
-    )
-    for copy in copies:
-        copy.start()
-    for copy in copies:
-        copy.wait()
+        block = slice(z * width, (z + 1) * width)
+        pltpu.make_async_copy(attended.at[:, block], attended_hbm.at[:, block], attended_sem).start()
+    pltpu.make_async_copy(attended, attended_hbm, attended_sem).wait()
+    logged_copy.wait()
 
 
 def on_device(queries, keys, values, page_lists, page_counts):
@@ -348,16 +353,16 @@
     tiles = n_head // sources
     groups = heads * tiles
     n_cross = n_cache // 2
-    cuts = tuple(sorted({0, min(1, heads), min(2, heads), min(4, heads), heads}))
+    cuts = tuple(sorted({0, min(1, heads), min(2, heads), min(3, heads), min(5, heads), heads}))
     batches = len(cuts) - 1
     plan = (heads, tiles, sources, n_head, n_cache, cuts)
     dma = pltpu.SemaphoreType.DMA
     anywhere = pl.BlockSpec(memory_space=pl.ANY)
-    attended, logged = pl.pallas_call(
+    pieces, logs = pl.pallas_call(
         functools.partial(kernel, plan),
         out_shape=(
-            pltpu.VMEM((share, queries.shape[1]), jnp.float32),
-            pltpu.VMEM((share, n_head * heads), jnp.float32),
+            pltpu.VMEM((n_cross * n_head, heads, share, DH), jnp.float32),
+            pltpu.VMEM((n_cross * n_head, LANES), jnp.float32),
         ),
         in_specs=[anywhere] * 5,
         out_specs=(pl.BlockSpec(memory_space=pltpu.VMEM), pl.BlockSpec(memory_space=pltpu.VMEM)),
@@ -372,9 +377,7 @@
             pltpu.VMEM((groups, 2, ROWS, LANES), jnp.float32),
             pltpu.VMEM((groups, ROWS, LANES), jnp.float32),
             pltpu.VMEM((groups, n_cross, sources, share, DH), jnp.float32),
-            pltpu.VMEM((n_cross * n_head, heads, share, DH), jnp.float32),
             pltpu.VMEM((tiles, n_cross * sources, LANES), jnp.float32),
-            pltpu.VMEM((n_cross * n_head, LANES), jnp.float32),
             dma(()),
             dma(()),
             dma((PREFETCH,)),
@@ -394,15 +397,17 @@
             collective_id=0, has_side_effects=True, vmem_limit_bytes=56 * 1024 * 1024
         ),
     )(queries, keys, values, page_lists, page_counts)
+    attended = jax.ShapeDtypeStruct((share, queries.shape[1]), jnp.float32)
+    logged = jax.ShapeDtypeStruct((share, n_head * heads), jnp.float32)
     return pl.pallas_call(
-        store,
-        out_shape=(
-            jax.ShapeDtypeStruct(attended.shape, jnp.float32), jax.ShapeDtypeStruct(logged.shape, jnp.float32)
-        ),
+        functools.partial(combine, plan),
+        out_shape=(attended, logged),
         in_specs=[pl.BlockSpec(memory_space=pltpu.VMEM)] * 2,
         out_specs=(anywhere, anywhere),
-        scratch_shapes=[dma(()), dma(())],
-    )(pltpu.with_memory_space_constraint(attended, pltpu.VMEM), pltpu.with_memory_space_constraint(logged, pltpu.VMEM))
+        scratch_shapes=[
+            pltpu.VMEM(attended.shape, jnp.float32), pltpu.VMEM(logged.shape, jnp.float32), dma(()), dma(())
+        ],
+    )(pltpu.with_memory_space_constraint(pieces, pltpu.VMEM), pltpu.with_memory_space_constraint(logs, pltpu.VMEM))
 
 
 def solution(mesh):

time: 30.3 us -> 30.2 us (level)
  no operation moved by 1% of the time
where the time goes in v5:
time: 30.2 us; the launch traced here: 30 us
  Pallas kernels  28.7 us (95%)
  between operations  1.29 us (4%)
    pallas_call x1, Pallas kernels, on_device(): pl.pallas_call(functools.partial(kernel, plan), out_shape=(pltpu.VMEM((n_...  27.6 us
    pallas_call x1, Pallas kernels, on_device(): pl.pallas_call(functools.partial(combine, plan), out_shape=(attended, log...  1.07 us

profile of v5, /device:TPU:0, one launch (start us, length us, event | category | flops | bytes accessed | tf_op | source)
XLA Modules:
  0.0 30.0 jit_solution(8151061651285733898)
XLA Ops:
  1.3 27.6 %shard_map.68 = (f32[8,8,16,128]{3,2,1,0:T(8,128)S(1)}, f32[8,128]{1,0:T(8,128)S(1)}) custom-call(bf16[64,4096]{1,0:T(8,128)(2,1)} %q_hbm.1, bf16[32,128,1024]{2,1,0:T(8,128)(2,1)} %k_hbm.1, bf16[32,128,1024]{2,1,0:T(8,128)(2,1)} %v_hbm.1, s32[1,32]{1,0:T(1,128)} %lists_hbm.1, s32[1]{0:T(128)S(6)} %copy.7.counts_hbm), custom_call_target="tpu_custom_call" | custom-call | tf_op jit(solution)/shard_map/pallas_call | solution.py:361
  28.9 1.1 %shard_map.69 = (f32[16,4096]{1,0:T(8,128)}, f32[16,32]{1,0:T(8,128)}) custom-call(f32[8,8,16,128]{3,2,1,0:T(8,128)S(1)} %get-tuple-element.4.piece_in, f32[8,128]{1,0:T(8,128)S(1)} %get-tuple-element.5.log_in), custom_call_target="tpu_custom_call" | custom-call | tf_op jit(solution)/shard_map/pallas_call | solution.py:402

commit v6 on v5

--- a/solution.py
+++ b/solution.py
@@ -185,10 +185,10 @@
     counts_copy = pltpu.make_async_copy(counts_hbm, counts, counts_sem)
     lists_copy.start()
     counts_copy.start()
+    load(0)
     pl.semaphore_wait(barrier, others + 1)
     for batch in range(min(3, batches)):
         send_queries(batch)
-    load(0)
     log_out[...] = jnp.zeros_like(log_out)
     lists_copy.wait()
     counts_copy.wait()
@@ -200,9 +200,9 @@
     caps[...] = jnp.broadcast_to(cap, caps.shape)
     for copy in own_copies:
         copy.wait()
+    arrive(0)
     for head in range(1, min(PREFETCH, heads)):
         load(head)
-    arrive(0)
     for batch in range(3, batches):
         send_queries(batch)
     if batches > 1:

time: 30.2 us -> 30.2 us (level)
  no operation moved by 1% of the time
where the time goes in v6:
time: 30.2 us; the launch traced here: 30 us
  Pallas kernels  28.7 us (95%)
  between operations  1.29 us (4%)
    pallas_call x1, Pallas kernels, on_device(): pl.pallas_call(functools.partial(kernel, plan), out_shape=(pltpu.VMEM((n_...  27.7 us
    pallas_call x1, Pallas kernels, on_device(): pl.pallas_call(functools.partial(combine, plan), out_shape=(attended, log...  1.07 us

profile of v6, /device:TPU:0, one launch (start us, length us, event | category | flops | bytes accessed | tf_op | source)
XLA Modules:
  0.0 30.0 jit_solution(17644251637073520654)
XLA Ops:
  1.3 27.7 %shard_map.68 = (f32[8,8,16,128]{3,2,1,0:T(8,128)S(1)}, f32[8,128]{1,0:T(8,128)S(1)}) custom-call(bf16[64,4096]{1,0:T(8,128)(2,1)} %q_hbm.1, bf16[32,128,1024]{2,1,0:T(8,128)(2,1)} %k_hbm.1, bf16[32,128,1024]{2,1,0:T(8,128)(2,1)} %v_hbm.1, s32[1,32]{1,0:T(1,128)} %lists_hbm.1, s32[1]{0:T(128)S(6)} %copy.7.counts_hbm), custom_call_target="tpu_custom_call" | custom-call | tf_op jit(solution)/shard_map/pallas_call | solution.py:361
  28.9 1.1 %shard_map.69 = (f32[16,4096]{1,0:T(8,128)}, f32[16,32]{1,0:T(8,128)}) custom-call(f32[8,8,16,128]{3,2,1,0:T(8,128)S(1)} %get-tuple-element.4.piece_in, f32[8,128]{1,0:T(8,128)S(1)} %get-tuple-element.5.log_in), custom_call_target="tpu_custom_call" | custom-call | tf_op jit(solution)/shard_map/pallas_call | solution.py:402
